TPU v7x, 512 devices: a whole 4x4x16 slice. The times are simulated.
512 devices in a mesh: section: 4 (over x), trial: 128 (over z, y, core).
Axes of the slice: x: 4, y: 4, z: 16, core: 2. Of those that a mesh axis runs over, the one named last changes fastest.
Arguments:
- spike_rates: bfloat16 [512, 256, 256], P(None, 'trial'), may hold values from -6 to 6
- first_preactivation: bfloat16 [1024, 256, 256], P('section', 'trial'), may hold values from -6 to 6
- second_preactivation: bfloat16 [1024, 256, 256], P('section', 'trial'), may hold values from -6 to 6
- output_gradient: bfloat16 [1024, 256, 256], P('section', 'trial'), may hold values from -0.29882812 to 0.29882812
- first_kernel: bfloat16 [3, 1024, 1024], P(None, None, 'section'), may hold values from -0.109375 to 0.109375
- second_kernel: bfloat16 [3, 1024, 1024], P(None, None, 'section'), may hold values from -0.109375 to 0.109375
- session_of: int32 [256], P('trial'), may hold values from 0 to 127, never falling along the last dimension, each value on 1 to 6 neighbouring positions
Outputs:
- readin_grad: bfloat16 [128, 512, 1024], P(None, 'trial', 'section')
Inputs may be any that keep to these rules, and one draw needn't show every extreme that they name: `session_of`: the trials of a session are consecutive; every session has 1 to 6 trials, and one has exactly 6.
All inputs are finite; a program needn't handle non-finite values.
Results may differ from a plain program's by a relative error of at most 0.017.
Values may be sent and summed in bfloat16 or wider, within the bound.
No kernel may reach another device: no remote copies, remote signals or barrier semaphores. Data moves between devices by JAX's collectives and lax.ppermute only.
A program may use at most 64 MiB of HBM per device.

v0:
```python
import math
import jax
import jax.numpy as jnp
from jax import lax
from jax.sharding import PartitionSpec as P

FIRST_DILATION = 32
SECOND_DILATION = 64
MOST = 6


def gelu_slope(preact):
    values = preact.astype(jnp.float32)
    normal_cdf = 0.5 * (1.0 + lax.erf(values * (1.0 / math.sqrt(2.0))))
    density = jnp.exp(-0.5 * values * values) * (1.0 / math.sqrt(2.0 * math.pi))
    return normal_cdf + values * density


def shift_ahead(values, offset):
    padding = [(0, 0)] * (values.ndim - 1) + [(0, offset)]
    return jnp.pad(values[..., offset:], padding)


def tap_sum(weights, flow_grad, spacing):
    running = None
    for kernel_tap in range(3):
        term_tap = lax.dot_general(
            weights[kernel_tap],
            flow_grad,
            (((1,), (0,)), ((), ())),
            preferred_element_type=jnp.float32,
        )
        if kernel_tap > 0:
            term_tap = shift_ahead(term_tap, kernel_tap * spacing)
        running = term_tap if running is None else running + term_tap
    return running


def layer_backprop(upstream, preact, turned, spacing):
    flow_grad = (upstream.astype(jnp.float32) * gelu_slope(preact)).astype(jnp.bfloat16)
    back_sum = tap_sum(turned, lax.all_gather(flow_grad, "section", axis=0, tiled=True), spacing)
    return (upstream.astype(jnp.float32) + back_sum).astype(jnp.bfloat16)


def body(
    spike_rates,
    first_preactivation,
    second_preactivation,
    output_gradient,
    first_kernel,
    second_kernel,
    session_of,
):
    first_flipped_kernel, second_flipped_kernel = (
        lax.all_to_all(first_kernel, "section", split_axis=1, concat_axis=2, tiled=True),
        lax.all_to_all(second_kernel, "section", split_axis=1, concat_axis=2, tiled=True),
    )
    upstream_gradient = layer_backprop(
        output_gradient, second_preactivation, second_flipped_kernel, SECOND_DILATION
    )
    input_gradient = layer_backprop(
        upstream_gradient, first_preactivation, first_flipped_kernel, FIRST_DILATION
    )
    trial_shards = lax.axis_size("trial")
    neurons, trials, steps_count = spike_rates.shape
    neuron_blocks = spike_rates.reshape(trial_shards, neurons // trial_shards, trials, steps_count)
    partials = jnp.einsum(
        "jbil,cil->jibc", neuron_blocks, input_gradient, preferred_element_type=jnp.float32
    )
    arrived = lax.all_to_all(
        partials.astype(jnp.bfloat16), "trial", split_axis=0, concat_axis=0, tiled=True
    ).astype(partials.dtype)
    every_id = lax.all_gather(session_of, "trial", axis=0, tiled=True)
    total_trials = every_id.shape[0]
    flat_parts = arrived.reshape(total_trials, -1)
    session_list = jnp.arange(trial_shards, dtype=jnp.int32)
    first_trial = jnp.sum((every_id[None, :] < session_list[:, None]).astype(jnp.int32), axis=1)

    def add_offset(offset, running):
        position = first_trial + offset
        clipped = jnp.minimum(position, total_trials - 1)
        rows_here = jnp.take(flat_parts, clipped, axis=0)
        valid = (position < total_trials) & (jnp.take(every_id, clipped, axis=0) == session_list)
        return running + jnp.where(valid[:, None], rows_here, 0.0)

    start_sums = jnp.zeros((trial_shards, flat_parts.shape[1]), jnp.float32)
    summed = lax.fori_loop(0, MOST, add_offset, start_sums)
    return summed.reshape(trial_shards, neurons // trial_shards, input_gradient.shape[0]).astype(
        jnp.bfloat16
    )


def solution(mesh):
    in_specs = (
        P(None, "trial", None),
        P("section", "trial", None),
        P("section", "trial", None),
        P("section", "trial", None),
        P(None, None, "section"),
        P(None, None, "section"),
        P("trial"),
    )
    out_specs = P(None, "trial", "section")
    return jax.shard_map(body, mesh=mesh, in_specs=in_specs, out_specs=out_specs, check_vma=False)
```

profile of v0, /device:TPU:8, one launch (start us, length us, event | category | flops | bytes accessed | tf_op | source)
XLA Modules:
  0.0 186.1 jit_solution(364001516441620479)
XLA Ops:
  6.5 1.2 copy.50
  9.9 2.7 %copy.52 = bf16[3,1024,256]{2,0,1:T(4,128)(2,1)} copy(bf16[3,1024,256]{2,1,0:T(8,128)(2,1)S(1)} %copy-done.3) | data formatting | bytes 3145728 | tf_op args[5]
  12.6 4.4 %all-to-all-start = ((bf16[3,1024,256]{2,0,1:T(4,128)(2,1)}), bf16[3,1024,256]{2,0,1:T(4,128)(2,1)S(1)}, u32[]{:S(2)}, u32[]{:S(2)}) async-start(bf16[3,1024,256]{2,0,1:T(4,128)(2,1)} %copy.52), calls=%async_computation | async-start | bytes 4194304 | tf_op jit(solution)/shard_map/all_to_all | solution.py:56
  17.2 29.0 %all-to-all-done = bf16[3,1024,256]{2,0,1:T(4,128)(2,1)S(1)} async-done(((bf16[3,1024,256]{2,0,1:T(4,128)(2,1)}), bf16[3,1024,256]{2,0,1:T(4,128)(2,1)S(1)}, u32[]{:S(2)}, u32[]{:S(2)}) %all-to-all-start) | async-done | bytes 1572896 | tf_op jit(solution)/shard_map/all_to_all | solution.py:56
  46.2 1.5 copy.79
  49.4 6.2 %all-gather.3.cloned.1.call-done = bf16[1024,2,256]{0,2,1:T(8,128)(2,1)} async-done(((bf16[256,2,256]{0,2,1:T(8,128)(2,1)}), bf16[1024,2,256]{0,2,1:T(8,128)(2,1)}) %all-gather.3.cloned.1.call-update) | async-done | bytes 1048592 | tf_op jit(solution)/shard_map/all_gather | solution.py:41
  55.6 1.8 convolution_bitcast_fusion.4
  57.9 1.5 fusion.31
  59.4 1.4 copy.55
  60.8 31.6 %all_to_all.35 = bf16[3,1024,256]{2,0,1:T(4,128)(2,1)S(1)} all-to-all(bf16[3,1024,256]{2,0,1:T(4,128)(2,1)S(1)} %copy.55), channel_id=1, replica_groups=mesh['section'=4,'trial'=128] {'section'}, dimensions={1} | all-to-all | bytes 3145728 | tf_op jit(solution)/shard_map/all_to_all | solution.py:55
  93.3 7.2 %all-gather.5.cloned.1.call-done = bf16[1024,2,256]{0,2,1:T(8,128)(2,1)} async-done(((bf16[256,2,256]{0,2,1:T(8,128)(2,1)}), bf16[1024,2,256]{0,2,1:T(8,128)(2,1)}) %all-gather.5.cloned.1.call-update) | async-done | bytes 1048592 | tf_op jit(solution)/shard_map/all_gather | solution.py:41
  100.5 1.8 convolution_bitcast_fusion.1
  102.8 2.0 %fusion.3 = bf16[128,2,4,256]{0,3,2,1:T(8,128)(2,1)S(1)} fusion(f32[256,2,256]{0,2,1:T(8,128)} %get-tuple-element.154, bf16[1024,2,256]{0,2,1:T(8,128)(2,1)S(1)} %copy-done.1, bf16[256,1024,1]{0,1,2:T(8,128)(2,1)S(1)} %bitcast.90, bf16[128,4,2,256]{3,2,1,0:T(2,128)(2,1)S(1)} %bitcast.84, f32[256,2,192]{0,2,1:T(8,128)S(1)} %slice.59, ...), kind=kOutput, calls=%fused_computation.13 | convolution fusion | flops 403439616 | bytes 3997696 | tf_op jit(solution)/shard_map/jbil,cil->jibc/dot_general | solution.py:67
  104.8 1.2 copy.65
  106.0 19.0 %all-to-all-start.2 = ((bf16[128,2,4,256]{3,2,1,0:T(4,128)(2,1)}), bf16[128,2,4,256]{3,2,1,0:T(4,128)(2,1)S(1)}, u32[]{:S(2)}, u32[]{:S(2)}) async-start(bf16[128,2,4,256]{3,2,1,0:T(4,128)(2,1)} %copy.65), calls=%async_computation.2 | async-start | bytes 1048576 | tf_op jit(solution)/shard_map/all_to_all | solution.py:70
  125.0 1.2 dynamic-slice
  127.1 37.2 %all-reduce.4 = s32[256]{0:T(256)S(1)} all-reduce(s32[256]{0:T(256)S(1)} %dynamic-update-slice), channel_id=1, replica_groups=mesh['section'=4,'trial'=128] {'trial'}, use_global_device_ids=true, to_apply=%add.4 | all-reduce | flops 256 | bytes 2048
  164.5 13.8 %while.14 = (s32[]{:T(128)}, f32[128,1024]{1,0:T(8,128)S(1)}, s32[128]{0:T(128)S(1)}, s32[256]{0:T(256)S(1)}, f32[256,1024]{1,0:T(8,128)S(1)}, /*index=5*/s32[]{:T(128)}, s32[]{:T(128)}) while((s32[]{:T(128)}, f32[128,1024]{1,0:T(8,128)S(1)}, s32[128]{0:T(128)S(1)}, s32[256]{0:T(256)S(1)}, f32[256,1024]{1,0:T(8,128)S(1)}, ...), condition=%wide.region_2.3_spmd.clone, body=%wide.region_1.2_spmd.clone.sunk | while | flops 527491 | bytes 2630751 | solution.py:87
  164.6 1.3 gather_fusion.1
  166.9 1.3 gather_fusion.1
  169.2 1.3 gather_fusion.1
  171.5 1.3 gather_fusion.1
  173.7 1.3 gather_fusion.1
  176.0 1.3 gather_fusion.1
  (74 shorter events, 13.1 us)
Async XLA Ops:
  6.5 96.3 %copy-start = (bf16[512,2,256]{2,1,0:T(2,128)(2,1)S(1)}, bf16[512,2,256]{2,1,0:T(2,128)(2,1)}, u32[]{:S(2)}) copy-start(bf16[512,2,256]{2,1,0:T(2,128)(2,1)} %param.9) | copy-start | bytes 1572868
  6.5 3.4 %copy-start.3 = (bf16[3,1024,256]{2,1,0:T(8,128)(2,1)S(1)}, bf16[3,1024,256]{2,1,0:T(8,128)(2,1)}, u32[]{:S(2)}) copy-start(bf16[3,1024,256]{2,1,0:T(8,128)(2,1)} %param.14) | copy-start | bytes 4718596
  6.5 49.0 %all-gather.3.cloned.1.call-start = ((), (), s32[]{:S(2)}) async-start(), calls=%async_computation.3 | async-start | bytes 1310720 | tf_op jit(solution)/shard_map/all_gather | solution.py:41
  12.6 4.4 %copy-start.5 = (bf16[256,2,256]{2,1,0:T(2,128)(2,1)S(1)}, bf16[256,2,256]{2,1,0:T(2,128)(2,1)}, u32[]{:S(2)}) copy-start(bf16[256,2,256]{2,1,0:T(2,128)(2,1)} %param.10) | copy-start | bytes 786436
  12.6 33.6 %all-to-all-start = ((bf16[3,1024,256]{2,0,1:T(4,128)(2,1)}), bf16[3,1024,256]{2,0,1:T(4,128)(2,1)S(1)}, u32[]{:S(2)}, u32[]{:S(2)}) async-start(bf16[3,1024,256]{2,0,1:T(4,128)(2,1)} %copy.52), calls=%async_computation | async-start | bytes 4194304 | tf_op jit(solution)/shard_map/all_to_all | solution.py:56
  17.0 83.5 %all-gather.5.cloned.1.call-start = ((), (), s32[]{:S(2)}) async-start(), calls=%async_computation.4 | async-start | bytes 1310720 | tf_op jit(solution)/shard_map/all_gather | solution.py:41
  55.6 1.8 copy-start.2
  57.9 1.5 copy-start.4
  100.5 1.8 copy-start.1
  104.8 22.1 %copy-start.6 = (s32[2]{0:T(128)S(1)}, s32[2]{0:T(128)}, u32[]{:S(2)}) copy-start(s32[2]{0:T(128)} %param.15) | copy-start | bytes 28
  106.0 58.4 %all-to-all-start.2 = ((bf16[128,2,4,256]{3,2,1,0:T(4,128)(2,1)}), bf16[128,2,4,256]{3,2,1,0:T(4,128)(2,1)S(1)}, u32[]{:S(2)}, u32[]{:S(2)}) async-start(bf16[128,2,4,256]{3,2,1,0:T(4,128)(2,1)} %copy.65), calls=%async_computation.2 | async-start | bytes 1048576 | tf_op jit(solution)/shard_map/all_to_all | solution.py:70
Sparse Core Ops, SparseCore 0:
  10.0 45.5 all-gather.2
  59.5 40.9 all-gather.4
where the time goes:
time: 187 us; the launch traced here: 186 us
  blocking collectives  68.8 us (37%)
  waiting for transfers between devices  42.5 us (23%)
  local copies, waits for them, and re-layouts  26.8 us (14%)
  starting transfers between devices  23.4 us (13%)
  between operations  14.2 us (8%)
  matrix products  7.88 us (4%)
  other arithmetic  2.14 us (1%)
    unnamed x1, blocking collectives  37.2 us
    all_to_all x1, blocking collectives, body(): lax.all_to_all(first_kernel, 'section', split_axis=1, concat_axis=2, tile...  31.6 us
    all_to_all x1, waiting for transfers between devices, body(): lax.all_to_all(second_kernel, 'section', split_axis=1, concat_axis=2, til...  29 us
    all_to_all x1, starting transfers between devices, body(): lax.all_to_all(partials.astype(jnp.bfloat16), 'trial', split_axis=0, conc...  19 us
    all_gather x2, waiting for transfers between devices, layer_backprop(): lax.all_gather(flow_grad, 'section', axis=0, tiled=True)  13.4 us
    unnamed x23, local copies, waits for them, and re-layouts  8.19 us
    gather x6, local copies, waits for them, and re-layouts, add_offset(): jnp.take(every_id, clipped, axis=0) == session_list  7.59 us
    dot_general x5, matrix products, tap_sum(): lax.dot_general(weights[kernel_tap], flow_grad, (((1,), (0,)), ((), ())),...  5.91 us
  transfers between devices with their start and end apart: 4, of which 3 were waited for; matrix products, arithmetic and copies ran while one was open for 5% of the time, Pallas kernels for 0%

commit v1 on v0

--- a/solution.py
+++ b/solution.py
@@ -1,3 +1,4 @@
+import functools
 import math
 import jax
 import jax.numpy as jnp
@@ -7,6 +8,21 @@
 FIRST_DILATION = 32
 SECOND_DILATION = 64
 MOST = 6
+
+
+def meet_field(local, chip_axis):
+    return jnp.concatenate(
+        jax.lax.all_to_all(
+            jnp.stack(tuple((local for _ in range(jax.lax.axis_size(chip_axis)))), axis=0),
+            chip_axis,
+            0,
+            0,
+        ),
+        axis=0,
+    )
+
+
+do_leaf = functools.partial(meet_field, chip_axis="section")
 
 
 def gelu_slope(preact):
@@ -38,7 +54,7 @@
 
 def layer_backprop(upstream, preact, turned, spacing):
     flow_grad = (upstream.astype(jnp.float32) * gelu_slope(preact)).astype(jnp.bfloat16)
-    back_sum = tap_sum(turned, lax.all_gather(flow_grad, "section", axis=0, tiled=True), spacing)
+    back_sum = tap_sum(turned, do_leaf(flow_grad), spacing)
     return (upstream.astype(jnp.float32) + back_sum).astype(jnp.bfloat16)
 
 

time: 187 us -> 180 us (0.963)
  blocking collectives: 68.8 us -> 37.1 us
  local copies, waits for them, and re-layouts: 26.8 us -> 43.6 us
  between operations: 14.2 us -> 0.95 us
  starting transfers between devices: 23.4 us -> 35.6 us
  waiting for transfers between devices: 42.5 us -> 52.1 us
    all_to_all x1 -> x0, blocking collectives: 31.6 us -> none  [body(): lax.all_to_all(first_kernel, 'section', split_axis=1, concat_axis=2, tile...]
    all_to_all x0 -> x3, waiting for transfers between devices: none -> 30.8 us  [the longest x2 19 us: meet_field(): jax.lax.all_to_all(jnp.stack(tuple((local for _ in range(jax.lax.axis_siz...]
    all_gather x2 -> x0, waiting for transfers between devices: 13.4 us -> none  [layer_backprop(): lax.all_gather(flow_grad, 'section', axis=0, tiled=True)]
    all_to_all x0 -> x3, starting transfers between devices: none -> 12.4 us  [the longest x2 7.99 us: meet_field(): jax.lax.all_to_all(jnp.stack(tuple((local for _ in range(jax.lax.axis_siz...]
    unnamed x23 -> x25, local copies, waits for them, and re-layouts: 8.19 us -> 16.5 us
    all_to_all x1, waiting for transfers between devices: 29 us -> 21.3 us  [body(): lax.all_to_all(second_kernel, 'section', split_axis=1, concat_axis=2, til...]
    another operation x0 -> x2, local copies, waits for them, and re-layouts: none -> 2.09 us  [meet_field(): jnp.stack(tuple((local for _ in range(jax.lax.axis_size(chip_axis)))), ax...]
  transfers between devices with their start and end apart: 4 -> 5, of which waited for: 3 -> 4; matrix products, arithmetic and copies ran while one was open for 5% -> 14% of each run, Pallas kernels for 0% -> 0%
where the time goes in v1:
time: 180 us; the launch traced here: 179 us
  waiting for transfers between devices  52.1 us (29%)
  local copies, waits for them, and re-layouts  43.6 us (24%)
  blocking collectives  37.1 us (21%)
  starting transfers between devices  35.6 us (20%)
  matrix products  8.35 us (5%)
    unnamed x1, blocking collectives  37.1 us
    all_to_all x1, waiting for transfers between devices, body(): lax.all_to_all(second_kernel, 'section', split_axis=1, concat_axis=2, til...  21.3 us
    all_to_all x1, starting transfers between devices, body(): lax.all_to_all(partials.astype(jnp.bfloat16), 'trial', split_axis=0, conc...  19.5 us
    all_to_all x2, waiting for transfers between devices, meet_field(): jax.lax.all_to_all(jnp.stack(tuple((local for _ in range(jax.lax.axis_siz...  19 us
    unnamed x25, local copies, waits for them, and re-layouts  16.5 us
    all_to_all x1, waiting for transfers between devices, body(): lax.all_to_all(first_kernel, 'section', split_axis=1, concat_axis=2, tile...  11.9 us
    all_to_all x2, starting transfers between devices, meet_field(): jax.lax.all_to_all(jnp.stack(tuple((local for _ in range(jax.lax.axis_siz...  7.99 us
    gather x6, local copies, waits for them, and re-layouts, add_offset(): jnp.take(every_id, clipped, axis=0) == session_list  7.59 us
  transfers between devices with their start and end apart: 5, of which 4 were waited for; matrix products, arithmetic and copies ran while one was open for 14% of the time, Pallas kernels for 0%

profile of v1, /device:TPU:8, one launch (start us, length us, event | category | flops | bytes accessed | tf_op | source)
XLA Modules:
  0.0 179.4 jit_solution(3173039155457711647)
XLA Ops:
  3.6 4.3 %all-to-all-start = ((bf16[4,256,2,256]{1,3,2,0:T(8,128)(2,1)}), bf16[4,256,2,256]{1,3,2,0:T(8,128)(2,1)S(1)}, u32[]{:S(2)}, u32[]{:S(2)}) async-start(bf16[4,256,2,256]{1,3,2,0:T(8,128)(2,1)} %stack.4), calls=%async_computation | async-start | bytes 2097152 | tf_op jit(solution)/shard_map/all_to_all | solution.py:15
  7.9 4.1 %copy.57 = bf16[3,1024,256]{2,0,1:T(4,128)(2,1)} copy(bf16[3,1024,256]{2,1,0:T(8,128)(2,1)} %param.14) | data formatting | bytes 3145728 | tf_op args[5]
  12.0 11.0 %all-to-all-done = bf16[4,256,2,256]{1,3,2,0:T(8,128)(2,1)S(1)} async-done(((bf16[4,256,2,256]{1,3,2,0:T(8,128)(2,1)}), bf16[4,256,2,256]{1,3,2,0:T(8,128)(2,1)S(1)}, u32[]{:S(2)}, u32[]{:S(2)}) %all-to-all-start) | async-done | bytes 1048608 | tf_op jit(solution)/shard_map/all_to_all | solution.py:15
  24.0 3.6 %all-to-all-start.1 = ((bf16[3,1024,256]{2,0,1:T(4,128)(2,1)}), bf16[3,1024,256]{2,0,1:T(4,128)(2,1)S(1)}, u32[]{:S(2)}, u32[]{:S(2)}) async-start(bf16[3,1024,256]{2,0,1:T(4,128)(2,1)} %copy.57), calls=%async_computation.1 | async-start | bytes 4194304 | tf_op jit(solution)/shard_map/all_to_all | solution.py:72
  27.6 4.1 %copy.61 = bf16[3,1024,256]{2,0,1:T(4,128)(2,1)} copy(bf16[3,1024,256]{2,1,0:T(8,128)(2,1)} %param.13) | data formatting | bytes 3145728 | tf_op args[4]
  31.7 21.3 %all-to-all-done.1 = bf16[3,1024,256]{2,0,1:T(4,128)(2,1)S(1)} async-done(((bf16[3,1024,256]{2,0,1:T(4,128)(2,1)}), bf16[3,1024,256]{2,0,1:T(4,128)(2,1)S(1)}, u32[]{:S(2)}, u32[]{:S(2)}) %all-to-all-start.1) | async-done | bytes 1572896 | tf_op jit(solution)/shard_map/all_to_all | solution.py:72
  53.0 1.4 copy-done.1
  54.3 4.4 %all-to-all-start.3 = ((bf16[3,1024,256]{2,0,1:T(4,128)(2,1)}), bf16[3,1024,256]{2,0,1:T(4,128)(2,1)}, u32[]{:S(2)}, u32[]{:S(2)}) async-start(bf16[3,1024,256]{2,0,1:T(4,128)(2,1)} %copy.61), calls=%async_computation.3 | async-start | bytes 4194304 | tf_op jit(solution)/shard_map/all_to_all | solution.py:71
  59.7 1.5 copy.81
  61.6 1.5 copy.87
  64.8 1.5 convolution_bitcast_fusion.4
  69.1 2.4 %fusion.31 = (bf16[256,2,256]{0,2,1:T(8,128)(2,1)S(1)}, f32[256,2,256]{0,2,1:T(8,128)}) fusion(bf16[256,2,256]{0,2,1:T(8,128)(2,1)} %copy.59, f32[256,2,128]{0,2,1:T(8,128)} %slice.54, f32[256,2,192]{0,2,1:T(8,128)S(1)} %slice-done, bf16[1024,2,256]{0,2,1:T(8,128)(2,1)S(1)} %bitcast.95, bf16[256,1024,1]{1,0,2:T(8,128)(2,1)S(1)} %reshape.116, ...), kind=kOutput, calls=%fused_computation.56 | convolution fusion | flops 270663680 | bytes 3538944 | tf_op jit(solution)/shard_map/dot_general | solution.py:43
  71.5 11.9 %all-to-all-done.3 = bf16[3,1024,256]{2,0,1:T(4,128)(2,1)} async-done(((bf16[3,1024,256]{2,0,1:T(4,128)(2,1)}), bf16[3,1024,256]{2,0,1:T(4,128)(2,1)}, u32[]{:S(2)}, u32[]{:S(2)}) %all-to-all-start.3) | async-done | bytes 1572896 | tf_op jit(solution)/shard_map/all_to_all | solution.py:71
  84.4 3.7 %all-to-all-start.2 = ((bf16[4,256,2,256]{1,3,2,0:T(8,128)(2,1)}), bf16[4,256,2,256]{1,3,2,0:T(8,128)(2,1)S(1)}, u32[]{:S(2)}, u32[]{:S(2)}) async-start(bf16[4,256,2,256]{1,3,2,0:T(8,128)(2,1)} %stack.5), calls=%async_computation.2 | async-start | bytes 2097152 | tf_op jit(solution)/shard_map/all_to_all | solution.py:15
  88.1 1.8 %copy.62 = bf16[3,1024,256]{2,1,0:T(8,128)(2,1)S(1)} copy(bf16[3,1024,256]{2,0,1:T(4,128)(2,1)} %all-to-all-done.3) | data formatting | bytes 3145728 | tf_op jit(solution)/shard_map/all_to_all | solution.py:71
  92.3 7.9 %all-to-all-done.2 = bf16[4,256,2,256]{1,3,2,0:T(8,128)(2,1)S(1)} async-done(((bf16[4,256,2,256]{1,3,2,0:T(8,128)(2,1)}), bf16[4,256,2,256]{1,3,2,0:T(8,128)(2,1)S(1)}, u32[]{:S(2)}, u32[]{:S(2)}) %all-to-all-start.2) | async-done | bytes 1048608 | tf_op jit(solution)/shard_map/all_to_all | solution.py:15
  100.3 1.5 convolution_bitcast_fusion.1
  102.5 2.0 %fusion.3 = bf16[128,2,4,256]{0,3,2,1:T(8,128)(2,1)S(1)} fusion(f32[256,2,256]{0,2,1:T(8,128)} %get-tuple-element.154, bf16[1024,2,256]{0,2,1:T(8,128)(2,1)S(1)} %bitcast.92, bf16[256,1024,1]{0,1,2:T(8,128)(2,1)S(1)} %bitcast.102, bf16[128,4,2,256]{3,2,1,0:T(2,128)(2,1)S(1)} %bitcast.88, f32[256,2,192]{0,2,1:T(8,128)S(1)} %slice.59, ...), kind=kOutput, calls=%fused_computation.13 | convolution fusion | flops 403439616 | bytes 3997696 | tf_op jit(solution)/shard_map/jbil,cil->jibc/dot_general | solution.py:83
  105.6 19.5 %all-to-all-start.4 = ((bf16[128,2,4,256]{3,2,1,0:T(4,128)(2,1)}), bf16[128,2,4,256]{3,2,1,0:T(4,128)(2,1)S(1)}, u32[]{:S(2)}, u32[]{:S(2)}) async-start(bf16[128,2,4,256]{3,2,1,0:T(4,128)(2,1)} %copy.71), calls=%async_computation.4 | async-start | bytes 1048576 | tf_op jit(solution)/shard_map/all_to_all | solution.py:86
  125.2 1.3 dynamic-slice
  127.4 37.1 %all-reduce.4 = s32[256]{0:T(256)S(1)} all-reduce(s32[256]{0:T(256)S(1)} %dynamic-update-slice), channel_id=1, replica_groups=mesh['section'=4,'trial'=128] {'trial'}, use_global_device_ids=true, to_apply=%add.4 | all-reduce | flops 256 | bytes 2048
  164.7 13.8 %while.14 = (s32[]{:T(128)}, f32[128,1024]{1,0:T(8,128)S(1)}, s32[128]{0:T(128)S(1)}, s32[256]{0:T(256)S(1)}, f32[256,1024]{1,0:T(8,128)S(1)}, /*index=5*/s32[]{:T(128)}, s32[]{:T(128)}) while((s32[]{:T(128)}, f32[128,1024]{1,0:T(8,128)S(1)}, s32[128]{0:T(128)S(1)}, s32[256]{0:T(256)S(1)}, f32[256,1024]{1,0:T(8,128)S(1)}, ...), condition=%wide.region_2.3_spmd.clone, body=%wide.region_1.2_spmd.clone.sunk | while | flops 527491 | bytes 2630751 | solution.py:103
  169.3 1.3 gather_fusion.1
  171.6 1.3 gather_fusion.1
  (80 shorter events, 27.8 us)
Async XLA Ops:
  0.0 102.4 %copy-start = (bf16[512,2,256]{2,1,0:T(2,128)(2,1)S(1)}, bf16[512,2,256]{2,1,0:T(2,128)(2,1)}, u32[]{:S(2)}) copy-start(bf16[512,2,256]{2,1,0:T(2,128)(2,1)} %param.9) | copy-start | bytes 1572868
  3.6 19.4 %all-to-all-start = ((bf16[4,256,2,256]{1,3,2,0:T(8,128)(2,1)}), bf16[4,256,2,256]{1,3,2,0:T(8,128)(2,1)S(1)}, u32[]{:S(2)}, u32[]{:S(2)}) async-start(bf16[4,256,2,256]{1,3,2,0:T(8,128)(2,1)} %stack.4), calls=%async_computation | async-start | bytes 2097152 | tf_op jit(solution)/shard_map/all_to_all | solution.py:15
  23.0 1.0 copy-start.3
  24.0 29.0 %all-to-all-start.1 = ((bf16[3,1024,256]{2,0,1:T(4,128)(2,1)}), bf16[3,1024,256]{2,0,1:T(4,128)(2,1)S(1)}, u32[]{:S(2)}, u32[]{:S(2)}) async-start(bf16[3,1024,256]{2,0,1:T(4,128)(2,1)} %copy.57), calls=%async_computation.1 | async-start | bytes 4194304 | tf_op jit(solution)/shard_map/all_to_all | solution.py:72
  31.7 27.1 %copy-start.6 = (bf16[256,2,256]{2,1,0:T(2,128)(2,1)S(1)}, bf16[256,2,256]{2,1,0:T(2,128)(2,1)}, u32[]{:S(2)}) copy-start(bf16[256,2,256]{2,1,0:T(2,128)(2,1)} %param.10) | copy-start | bytes 786436
  53.0 1.4 copy-start.1
  54.3 29.0 %all-to-all-start.3 = ((bf16[3,1024,256]{2,0,1:T(4,128)(2,1)}), bf16[3,1024,256]{2,0,1:T(4,128)(2,1)}, u32[]{:S(2)}, u32[]{:S(2)}) async-start(bf16[3,1024,256]{2,0,1:T(4,128)(2,1)} %copy.61), calls=%async_computation.3 | async-start | bytes 4194304 | tf_op jit(solution)/shard_map/all_to_all | solution.py:71
  59.7 1.9 %copy-start.2 = (bf16[3,1024,256]{2,0,1:T(4,128)(2,1)S(1)}, bf16[3,1024,256]{2,0,1:T(4,128)(2,1)}, u32[]{:S(2)}) copy-start(bf16[3,1024,256]{2,0,1:T(4,128)(2,1)} %copy-done.1) | copy-start | bytes 4718596
  66.3 0.8 copy-start.5
  67.5 1.6 slice-start
  84.4 15.8 %all-to-all-start.2 = ((bf16[4,256,2,256]{1,3,2,0:T(8,128)(2,1)}), bf16[4,256,2,256]{1,3,2,0:T(8,128)(2,1)S(1)}, u32[]{:S(2)}, u32[]{:S(2)}) async-start(bf16[4,256,2,256]{1,3,2,0:T(8,128)(2,1)} %stack.5), calls=%async_computation.2 | async-start | bytes 2097152 | tf_op jit(solution)/shard_map/all_to_all | solution.py:15
  100.3 1.6 copy-start.4
  104.4 22.7 %copy-start.7 = (s32[2]{0:T(128)S(1)}, s32[2]{0:T(128)}, u32[]{:S(2)}) copy-start(s32[2]{0:T(128)} %param.15) | copy-start | bytes 28
  105.6 58.9 %all-to-all-start.4 = ((bf16[128,2,4,256]{3,2,1,0:T(4,128)(2,1)}), bf16[128,2,4,256]{3,2,1,0:T(4,128)(2,1)S(1)}, u32[]{:S(2)}, u32[]{:S(2)}) async-start(bf16[128,2,4,256]{3,2,1,0:T(4,128)(2,1)} %copy.71), calls=%async_computation.4 | async-start | bytes 1048576 | tf_op jit(solution)/shard_map/all_to_all | solution.py:86
